TPU v7x, 128 devices: a whole 4x4x4 slice. The times are simulated.
128 devices in a mesh: layer: 8 (over z_hi, x), feat: 16 (over z_lo, y, core).
Axes of the slice: x: 4, y: 4, z: 4 (z_hi: 2, z_lo: 2; z = z_hi * 2 + z_lo), core: 2. Of those that a mesh axis runs over, the one named last changes fastest.
Arguments:
- activations: bfloat16 [4, 1024, 32768], P(None, None, ('layer', 'feat')), may hold values from -6 to 6
- active_blocks: int32 [4, 1024, 256], P(None, None, ('layer', 'feat')), may hold values from 0 to 1, as said below
- cotangent: bfloat16 [4, 1024, 2048], P(None, 'layer', 'feat'), may hold values from -6 to 6
- decoder: bfloat16 [10, 32768, 2048], P(None, ('layer', 'feat')), may hold values from -0.03125 to 0.03125
Outputs:
- decoder_grad: bfloat16 [10, 32768, 2048], P(None, ('layer', 'feat'))
- feature_grad: bfloat16 [4, 1024, 32768], P(None, None, ('layer', 'feat'))
Inputs may be any that keep to these rules, and one draw needn't show every extreme that they name: `active_blocks`: 1 where the block of 128 features is active for that token at that layer, else 0.
All inputs are finite; a program needn't handle non-finite values.
Results may differ from a plain program's by a relative error of at most 0.001.
Values may be sent and summed in bfloat16 or wider, within the bound.
A program may use at most 128 MiB of HBM per device.

v0:
```python
import jax
import jax.numpy as jnp
from jax import lax
from jax.sharding import PartitionSpec as P


def pair_work(sparse, upstream, weights, layers):
    grads = []
    partial_value = jnp.zeros((layers, sparse.shape[1], sparse.shape[2]), jnp.float32)
    offset = 0
    for target in range(layers):
        count = target + 1
        rows = weights[offset : offset + count]
        grads.append(
            jnp.einsum(
                "stf,td->sfd", sparse[:count], upstream[target], preferred_element_type=jnp.float32
            )
        )
        terms = jnp.einsum(
            "td,sfd->stf", upstream[target], rows, preferred_element_type=jnp.float32
        )
        partial_value = partial_value.at[:count].add(terms)
        offset = offset + count
    return (jnp.concatenate(grads, axis=0), partial_value)


def body(activations, active_blocks, cotangent, decoder):
    width = activations.shape[2] // active_blocks.shape[2]
    layers = activations.shape[0]
    feature_mask = jnp.repeat(active_blocks, width, axis=2).astype(jnp.float32)
    sparse = (activations.astype(jnp.float32) * feature_mask).astype(jnp.bfloat16)
    cot_rows = lax.all_gather(cotangent, "layer", axis=1, tiled=True)
    upstream = lax.all_gather(cot_rows, "feat", axis=2, tiled=True)
    weight_grads, partial_value = pair_work(sparse, upstream, decoder, layers)
    feature_grad = (partial_value * feature_mask).astype(jnp.bfloat16)
    return (weight_grads.astype(jnp.bfloat16), feature_grad)


def solution(mesh):
    in_specs = (
        P(None, None, ("layer", "feat")),
        P(None, None, ("layer", "feat")),
        P(None, "layer", "feat"),
        P(None, ("layer", "feat"), None),
    )
    out_specs = (P(None, ("layer", "feat"), None), P(None, None, ("layer", "feat")))
    return jax.shard_map(body, mesh=mesh, in_specs=in_specs, out_specs=out_specs, check_vma=False)
```

profile of v0, /device:TPU:1, one launch (start us, length us, event | category | flops | bytes accessed | tf_op | source)
XLA Modules:
  0.0 217.0 jit_solution(17988041659607771263)
XLA Ops:
  7.2 0.0 all-gather.3.cloned.1.call-start
  7.2 0.7 all-gather.3.cloned.1.call-update
  7.9 0.0 all-gather.5.cloned.1.call-start
  7.9 51.1 %all-gather.3.cloned.1.call-done = bf16[4,1024,128]{2,1,0:T(8,128)(2,1)} async-done(((bf16[4,128,128]{2,1,0:T(8,128)(2,1)}), bf16[4,1024,128]{2,1,0:T(8,128)(2,1)}) %all-gather.3.cloned.1.call-update) | async-done | bytes 1048592 | tf_op jit(solution)/shard_map/all_gather | solution.py:32
  59.1 0.0 all-gather.5.cloned.1.call-update
  59.1 0.8 convert_element_type.18
  59.9 3.0 %copy.6 = bf16[4,1024,256]{1,2,0:T(8,128)(2,1)S(1)} copy(bf16[4,1024,256]{2,1,0:T(8,128)(2,1)} %param.14) | data formatting | bytes 4194304 | tf_op args[0]
  62.9 1.9 fusion
  64.8 94.6 %all-gather.5.cloned.1.call-done = bf16[4,1024,2048]{2,1,0:T(8,128)(2,1)} async-done(((bf16[4,1024,128]{2,1,0:T(8,128)(2,1)}), bf16[4,1024,2048]{2,1,0:T(8,128)(2,1)}) %all-gather.5.cloned.1.call-update) | async-done | bytes 16777232 | tf_op jit(solution)/shard_map/all_gather | solution.py:33
  159.4 3.8 %fusion.15 = f32[1,1024,256]{1,2,0:T(8,128)S(1)} fusion(bf16[4,1024,2048]{2,1,0:T(8,128)(2,1)} %all-gather.5.cloned.1.call-done, bf16[10,256,2048]{2,1,0:T(8,128)(2,1)} %param.17), kind=kOutput, calls=%fused_computation.26 | convolution fusion | flops 1073741824 | bytes 6291456 | tf_op jit(solution)/shard_map/td,sfd->stf/dot_general | solution.py:19
  163.2 0.0 slice-start
  163.2 0.5 scatter-add.10
  163.7 0.0 slice-start.1
  163.7 0.0 slice-start.2
  163.7 5.6 %fusion.14 = f32[4,1024,256]{1,2,0:T(8,128)S(1)} fusion(f32[4,1024,256]{1,2,0:T(8,128)S(1)} %scatter-add.10, bf16[10,256,2048]{2,1,0:T(8,128)(2,1)} %param.17, bf16[4,1024,2048]{2,1,0:T(8,128)(2,1)} %all-gather.5.cloned.1.call-done), kind=kOutput, calls=%fused_computation.25 | convolution fusion | flops 2148007936 | bytes 18874368 | tf_op jit(solution)/shard_map/td,sfd->stf/dot_general | solution.py:19
  169.4 0.0 slice-done
  169.4 0.0 slice-done.1
  169.4 0.0 slice-done.2
  169.4 5.5 %fusion.10 = f32[4,1024,256]{1,2,0:T(8,128)S(1)} fusion(f32[4,1024,256]{1,2,0:T(8,128)S(1)} %fusion.14, bf16[10,256,2048]{2,1,0:T(8,128)(2,1)S(1)} %bitcast.71, bf16[4,1024,2048]{2,1,0:T(8,128)(2,1)} %all-gather.5.cloned.1.call-done), kind=kOutput, calls=%fused_computation.20 | convolution fusion | flops 3222011904 | bytes 20971520 | tf_op jit(solution)/shard_map/td,sfd->stf/dot_general | solution.py:19
  174.9 7.0 %fusion.1 = bf16[4,1024,256]{1,2,0:T(8,128)(2,1)S(1)} fusion(f32[4,1024,256]{1,2,0:T(8,128)S(1)} %fusion.10, f32[4,1024,2]{1,2,0:T(2,128)S(1)} %convert_element_type.18, bf16[10,256,2048]{2,1,0:T(8,128)(2,1)S(1)} %bitcast.71, bf16[4,1024,2048]{2,1,0:T(8,128)(2,1)} %all-gather.5.cloned.1.call-done), kind=kOutput, calls=%fused_computation.4 | convolution fusion | flops 4298113024 | bytes 21004288 | tf_op jit(solution)/shard_map/td,sfd->stf/dot_general | solution.py:19
  181.9 2.6 %copy.7 = bf16[4,1024,256]{2,1,0:T(8,128)(2,1)} copy(bf16[4,1024,256]{1,2,0:T(8,128)(2,1)S(1)} %fusion.1) | data formatting | bytes 4194304
  184.4 7.5 %convolution_convert_fusion = bf16[4,256,2048]{2,1,0:T(8,128)(2,1)S(1)} fusion(bf16[4,1024,256]{1,2,0:T(8,128)(2,1)} %fusion, bf16[4,1024,2048]{2,1,0:T(8,128)(2,1)} %all-gather.5.cloned.1.call-done), kind=kOutput, calls=%fused_computation.10 | convolution fusion | flops 4297064448 | bytes 10485760 | tf_op jit(solution)/shard_map/stf,td->sfd/dot_general | solution.py:15
  191.9 0.0 copy-done
  191.9 0.0 slice-start.6
  191.9 6.2 %fusion.9 = bf16[3,256,2048]{2,1,0:T(8,128)(2,1)S(1)} fusion(bf16[4,1024,256]{1,2,0:T(8,128)(2,1)S(1)} %copy-done, bf16[4,1024,2048]{2,1,0:T(8,128)(2,1)} %all-gather.5.cloned.1.call-done), kind=kOutput, calls=%fused_computation.18 | convolution fusion | flops 3222798336 | bytes 9437184 | tf_op jit(solution)/shard_map/stf,td->sfd/dot_general | solution.py:15
  198.1 0.0 slice-done.3
  198.1 0.0 slice-done.4
  198.1 0.0 slice-done.5
  198.1 0.0 slice-done.6
  198.1 2.4 %fusion.11 = bf16[2,256,2048]{2,1,0:T(8,128)(2,1)S(1)} fusion(bf16[4,1024,256]{1,2,0:T(8,128)(2,1)S(1)} %copy-done, bf16[4,1024,2048]{2,1,0:T(8,128)(2,1)S(1)} %bitcast.73), kind=kOutput, calls=%fused_computation.21 | convolution fusion | flops 2148532224 | bytes 8388608 | tf_op jit(solution)/shard_map/stf,td->sfd/dot_general | solution.py:15
  200.5 1.3 fusion.13
  201.8 8.4 %pad_maximum_fusion = bf16[10,256,2048]{2,1,0:T(8,128)(2,1)} fusion(bf16[4,256,2048]{2,1,0:T(8,128)(2,1)S(1)} %convolution_convert_fusion, bf16[3,256,2048]{2,1,0:T(8,128)(2,1)S(1)} %fusion.9, bf16[2,256,2048]{2,1,0:T(8,128)(2,1)S(1)} %fusion.11, bf16[1,256,2048]{2,1,0:T(8,128)(2,1)S(1)} %fusion.13), kind=kLoop, calls=%fused_computation | loop fusion | flops 15728640 | bytes 20971520 | tf_op jit(solution)/shard_map/concatenate | solution.py:24
  (6 shorter events, 0.0 us)
Async XLA Ops:
  7.2 51.9 %all-gather.3.cloned.1.call-start = ((), (), s32[]{:S(2)}) async-start(), calls=%async_computation | async-start | bytes 1179648 | tf_op jit(solution)/shard_map/all_gather | solution.py:32
  7.9 151.5 %all-gather.5.cloned.1.call-start = ((), (), s32[]{:S(2)}) async-start(), calls=%async_computation.1 | async-start | bytes 17825792 | tf_op jit(solution)/shard_map/all_gather | solution.py:33
  163.2 6.2 %slice-start = ((s8[10485760]{0:T(1024)(128)(4,1)}), s8[4194304]{0:T(1024)(128)(4,1)S(1)}, s32[]{:S(2)}) async-start(s8[10485760]{0:T(1024)(128)(4,1)} %bitcast.70), calls=%async_computation.2 | async-start | bytes 8388608
  163.7 5.7 %slice-start.1 = ((s8[10485760]{0:T(1024)(128)(4,1)}), s8[4194304]{0:T(1024)(128)(4,1)S(1)}, s32[]{:S(2)}) async-start(s8[10485760]{0:T(1024)(128)(4,1)} %bitcast.70), calls=%async_computation.3 | async-start | bytes 8388608
  163.7 5.7 %slice-start.2 = ((s8[10485760]{0:T(1024)(128)(4,1)}), s8[2097152]{0:T(1024)(128)(4,1)S(1)}, s32[]{:S(2)}) async-start(s8[10485760]{0:T(1024)(128)(4,1)} %bitcast.70), calls=%async_computation.4 | async-start | bytes 4194304
  184.4 7.5 %copy-start = (bf16[4,1024,256]{1,2,0:T(8,128)(2,1)S(1)}, bf16[4,1024,256]{1,2,0:T(8,128)(2,1)}, u32[]{:S(2)}) copy-start(bf16[4,1024,256]{1,2,0:T(8,128)(2,1)} %fusion) | copy-start | bytes 6291460
  184.4 13.7 %slice-start.3 = ((s8[16777216]{0:T(1024)(128)(4,1)}), s8[4194304]{0:T(1024)(128)(4,1)S(1)}, s32[]{:S(2)}) async-start(s8[16777216]{0:T(1024)(128)(4,1)} %bitcast.72), calls=%async_computation.5 | async-start | bytes 8388608
  184.4 13.7 %slice-start.4 = ((s8[16777216]{0:T(1024)(128)(4,1)}), s8[4194304]{0:T(1024)(128)(4,1)S(1)}, s32[]{:S(2)}) async-start(s8[16777216]{0:T(1024)(128)(4,1)} %bitcast.72), calls=%async_computation.6 | async-start | bytes 8388608
  184.4 13.7 %slice-start.5 = ((s8[16777216]{0:T(1024)(128)(4,1)}), s8[4194304]{0:T(1024)(128)(4,1)S(1)}, s32[]{:S(2)}) async-start(s8[16777216]{0:T(1024)(128)(4,1)} %bitcast.72), calls=%async_computation.7 | async-start | bytes 8388608
  191.9 6.2 %slice-start.6 = ((s8[16777216]{0:T(1024)(128)(4,1)}), s8[4194304]{0:T(1024)(128)(4,1)S(1)}, s32[]{:S(2)}) async-start(s8[16777216]{0:T(1024)(128)(4,1)} %bitcast.72), calls=%async_computation.8 | async-start | bytes 8388608
Sparse Core Ops, SparseCore 0:
  10.3 48.6 all-gather.2
  60.7 98.6 all-gather.4
where the time goes:
time: 217 us
  waiting for transfers between devices  146 us (67%)
  matrix products  39.1 us (18%)
  between operations  14.2 us (7%)
  other arithmetic  11 us (5%)
  local copies, waits for them, and re-layouts  6.11 us (3%)
    all_gather x1, waiting for transfers between devices, body(): upstream = lax.all_gather(cot_rows, 'feat', axis=2, tiled=True)  94.6 us
    all_gather x1, waiting for transfers between devices, body(): cot_rows = lax.all_gather(cotangent, 'layer', axis=1, tiled=True)  51.1 us
    dot_general x4, matrix products, pair_work(): jnp.einsum('td,sfd->stf', upstream[target], rows, preferred_element_type=...  21.9 us
    dot_general x4, matrix products, pair_work(): jnp.einsum('stf,td->sfd', sparse[:count], upstream[target], preferred_ele...  17.3 us
    concatenate x1, other arithmetic, pair_work(): return (jnp.concatenate(grads, axis=0), partial_value)  8.37 us
    unnamed x18, local copies, waits for them, and re-layouts  5.6 us
  transfers between devices with their start and end apart: 2, of which 2 were waited for; matrix products, arithmetic and copies ran while one was open for 3% of the time, Pallas kernels for 0%

commit v1 on v0

--- a/solution.py
+++ b/solution.py
@@ -30,7 +30,10 @@
     feature_mask = jnp.repeat(active_blocks, width, axis=2).astype(jnp.float32)
     sparse = (activations.astype(jnp.float32) * feature_mask).astype(jnp.bfloat16)
     cot_rows = lax.all_gather(cotangent, "layer", axis=1, tiled=True)
-    upstream = lax.all_gather(cot_rows, "feat", axis=2, tiled=True)
+    size = lax.axis_size("feat")
+    shards = jnp.stack([cot_rows for _ in range(size)])
+    shards = lax.all_to_all(shards, "feat", split_axis=0, concat_axis=0)
+    upstream = jnp.concatenate(shards, axis=2)
     weight_grads, partial_value = pair_work(sparse, upstream, decoder, layers)
     feature_grad = (partial_value * feature_mask).astype(jnp.bfloat16)
     return (weight_grads.astype(jnp.bfloat16), feature_grad)

time: 217 us -> 380 us (1.75)
  waiting for transfers between devices: 146 us -> 271 us
  local copies, waits for them, and re-layouts: 6.11 us -> 44.7 us
  matrix products: 39.1 us -> 30.7 us
  starting transfers between devices: 0.08 us -> 7.3 us
    all_to_all x0 -> x1, waiting for transfers between devices: none -> 219 us  [body(): shards = lax.all_to_all(shards, 'feat', split_axis=0, concat_axis=0)]
    all_gather x1 -> x0, waiting for transfers between devices: 94.6 us -> none  [body(): upstream = lax.all_gather(cot_rows, 'feat', axis=2, tiled=True)]
    all_to_all x0 -> x1, local copies, waits for them, and re-layouts: none -> 22.6 us  [body(): shards = lax.all_to_all(shards, 'feat', split_axis=0, concat_axis=0)]
    slice x0 -> x1, local copies, waits for them, and re-layouts: none -> 8.91 us  [pair_work(): upstream[target]]
    dot_general x4, matrix products: 21.9 us -> 13.6 us  [pair_work(): jnp.einsum('td,sfd->stf', upstream[target], rows, preferred_element_type=...]
    all_to_all x0 -> x1, starting transfers between devices: none -> 7.26 us  [body(): shards = lax.all_to_all(shards, 'feat', split_axis=0, concat_axis=0)]
    another operation x0 -> x1, local copies, waits for them, and re-layouts: none -> 7.03 us  [body(): shards = jnp.stack([cot_rows for _ in range(size)])]
  transfers between devices with their start and end apart: 2 -> 2, of which waited for: 2 -> 2; matrix products, arithmetic and copies ran while one was open for 3% -> 1% of each run, Pallas kernels for 0% -> 0%
where the time goes in v1:
time: 380 us; the launch traced here: 379 us
  waiting for transfers between devices  271 us (71%)
  local copies, waits for them, and re-layouts  44.7 us (12%)
  matrix products  30.7 us (8%)
  between operations  14.2 us (4%)
  other arithmetic  10.9 us (3%)
  starting transfers between devices  7.3 us (2%)
    all_to_all x1, waiting for transfers between devices, body(): shards = lax.all_to_all(shards, 'feat', split_axis=0, concat_axis=0)  219 us
    all_gather x1, waiting for transfers between devices, body(): cot_rows = lax.all_gather(cotangent, 'layer', axis=1, tiled=True)  51.2 us
    all_to_all x1, local copies, waits for them, and re-layouts, body(): shards = lax.all_to_all(shards, 'feat', split_axis=0, concat_axis=0)  22.6 us
    dot_general x4, matrix products, pair_work(): jnp.einsum('stf,td->sfd', sparse[:count], upstream[target], preferred_ele...  17.1 us
    dot_general x4, matrix products, pair_work(): jnp.einsum('td,sfd->stf', upstream[target], rows, preferred_element_type=...  13.6 us
    concatenate x1, other arithmetic, pair_work(): return (jnp.concatenate(grads, axis=0), partial_value)  9.03 us
    slice x1, local copies, waits for them, and re-layouts, pair_work(): upstream[target]  8.91 us
  transfers between devices with their start and end apart: 2, of which 2 were waited for; matrix products, arithmetic and copies ran while one was open for 1% of the time, Pallas kernels for 0%

profile of v1, /device:TPU:1, one launch (start us, length us, event | category | flops | bytes accessed | tf_op | source)
XLA Modules:
  0.0 378.8 jit_solution(17059909106581690044)
XLA Ops:
  7.2 0.0 all-gather.2.cloned.1.call-start
  7.2 0.7 all-gather.2.cloned.1.call-update
  7.9 51.2 %all-gather.2.cloned.1.call-done = bf16[4,1024,128]{2,1,0:T(8,128)(2,1)} async-done(((bf16[4,128,128]{2,1,0:T(8,128)(2,1)}), bf16[4,1024,128]{2,1,0:T(8,128)(2,1)}) %all-gather.2.cloned.1.call-update) | async-done | bytes 1048592 | tf_op jit(solution)/shard_map/all_gather | solution.py:32
  59.1 7.0 %stack.2 = bf16[16,4,1024,128]{3,2,1,0:T(8,128)(2,1)} broadcast(bf16[4,1024,128]{2,1,0:T(8,128)(2,1)} %all-gather.2.cloned.1.call-done), dimensions={1,2,3} | broadcast | bytes 17825792 | tf_op jit(solution)/shard_map/stack | solution.py:34
  66.1 0.0 copy-start.4
  66.1 7.3 %all-to-all-start = ((bf16[16,4,1024,128]{3,2,1,0:T(8,128)(2,1)}), bf16[16,4,1024,128]{3,2,1,0:T(8,128)(2,1)}, u32[]{:S(2)}, u32[]{:S(2)}) async-start(bf16[16,4,1024,128]{3,2,1,0:T(8,128)(2,1)} %stack.2), calls=%async_computation | async-start | bytes 33554432 | tf_op jit(solution)/shard_map/all_to_all | solution.py:35
  73.4 0.0 copy-done.4
  73.4 3.0 copy.13
  76.4 1.9 fusion
  78.3 219.3 %all-to-all-done = bf16[16,4,1024,128]{3,2,1,0:T(8,128)(2,1)} async-done(((bf16[16,4,1024,128]{3,2,1,0:T(8,128)(2,1)}), bf16[16,4,1024,128]{3,2,1,0:T(8,128)(2,1)}, u32[]{:S(2)}, u32[]{:S(2)}) %all-to-all-start) | async-done | bytes 16777248 | tf_op jit(solution)/shard_map/all_to_all | solution.py:35
  297.5 22.6 %copy.14 = bf16[16,4,1024,128]{2,3,0,1:T(8,128)(2,1)} copy(bf16[16,4,1024,128]{3,2,1,0:T(8,128)(2,1)} %all-to-all-done) | data formatting | bytes 33554432 | tf_op jit(solution)/shard_map/all_to_all | solution.py:35
  320.2 8.9 %fusion.7 = (bf16[1,1024,16,128]{1,3,2,0:T(8,128)(2,1)S(1)}, bf16[1,1024,16,128]{1,3,2,0:T(8,128)(2,1)S(1)}, bf16[1,1024,16,128]{1,3,2,0:T(8,128)(2,1)S(1)}, bf16[1,1024,16,128]{1,3,2,0:T(8,128)(2,1)}) fusion(bf16[4,1024,16,128]{1,3,2,0:T(8,128)(2,1)} %bitcast.60), kind=kLoop, calls=%fused_computation.19 | loop fusion | bytes 33554432 | tf_op jit(solution)/shard_map/slice | solution.py:16
  329.1 2.7 convolution_bitcast_fusion
  331.8 0.0 copy-done.1
  331.8 0.0 slice-start
  331.8 2.3 fusion.3
  334.0 0.0 copy-done
  334.1 3.8 %convolution_convert_fusion.2 = bf16[2,256,2048]{2,1,0:T(8,128)(2,1)} fusion(bf16[4,1024,256]{1,2,0:T(8,128)(2,1)S(1)} %copy-done.1, bf16[1024,2048,1]{0,1,2:T(8,128)(2,1)S(1)} %bitcast.67), kind=kOutput, calls=%fused_computation.10 | convolution fusion | flops 2148532224 | bytes 8388608 | tf_op jit(solution)/shard_map/stf,td->sfd/dot_general | solution.py:15
  337.9 0.5 scatter-add.10
  338.4 0.0 slice-done
  338.4 0.0 slice-done.1
  338.4 0.0 slice-done.2
  338.4 2.5 fusion.4
  340.9 4.9 %convolution_convert_fusion.1 = bf16[3,256,2048]{2,1,0:T(8,128)(2,1)} fusion(bf16[4,1024,256]{1,2,0:T(8,128)(2,1)S(1)} %copy-done.1, bf16[1024,2048,1]{0,1,2:T(8,128)(2,1)S(1)} %bitcast.65), kind=kOutput, calls=%fused_computation.7 | convolution fusion | flops 3222798336 | bytes 9437184 | tf_op jit(solution)/shard_map/stf,td->sfd/dot_general | solution.py:15
  345.8 3.7 fusion.2
  349.5 0.0 copy-done.2
  349.5 6.1 %convolution_convert_fusion = bf16[4,256,2048]{2,1,0:T(8,128)(2,1)} fusion(bf16[4,1024,256]{1,2,0:T(8,128)(2,1)S(1)} %copy-done.2, bf16[1024,2048,1]{0,1,2:T(8,128)(2,1)S(1)} %bitcast.61), kind=kOutput, calls=%fused_computation.6 | convolution fusion | flops 4297064448 | bytes 10485760 | tf_op jit(solution)/shard_map/stf,td->sfd/dot_general | solution.py:15
  355.6 4.7 %fusion.1 = bf16[4,1024,256]{1,2,0:T(8,128)(2,1)S(1)} fusion(f32[4,1024,256]{1,2,0:T(8,128)S(1)} %fusion.2, bf16[10,256,2048]{2,1,0:T(8,128)(2,1)S(1)} %bitcast.64, bf16[1024,2048,1]{0,1,2:T(8,128)(2,1)S(1)} %bitcast.62, f32[4,1024,2]{1,2,0:T(2,128)S(1)} %convert_element_type.18), kind=kOutput, calls=%fused_computation.4 | convolution fusion | flops 4298113024 | bytes 21004288 | tf_op jit(solution)/shard_map/td,sfd->stf/dot_general | solution.py:19
  360.4 0.0 copy-start.3
  360.4 2.6 copy.18
  362.9 0.0 copy-done.3
  363.0 9.0 %pad_maximum_fusion = bf16[10,256,2048]{2,1,0:T(8,128)(2,1)} fusion(bf16[4,256,2048]{2,1,0:T(8,128)(2,1)} %convolution_convert_fusion, bf16[3,256,2048]{2,1,0:T(8,128)(2,1)} %convolution_convert_fusion.1, bf16[2,256,2048]{2,1,0:T(8,128)(2,1)} %convolution_convert_fusion.2, bf16[1,256,2048]{2,1,0:T(8,128)(2,1)S(1)} %copy-done.3), kind=kLoop, calls=%fused_computation | loop fusion | flops 15728640 | bytes 20971520 | tf_op jit(solution)/shard_map/concatenate | solution.py:24
  (7 shorter events, 0.0 us)
Async XLA Ops:
  7.2 51.9 %all-gather.2.cloned.1.call-start = ((), (), s32[]{:S(2)}) async-start(), calls=%async_computation.1 | async-start | bytes 1179648 | tf_op jit(solution)/shard_map/all_gather | solution.py:32
  66.1 7.3 %copy-start.4 = (s32[4,1024,2]{1,2,0:T(2,128)S(1)}, s32[4,1024,2]{1,2,0:T(2,128)}, u32[]{:S(2)}) copy-start(s32[4,1024,2]{1,2,0:T(2,128)} %param.15) | copy-start | bytes 98308
  66.1 231.5 %all-to-all-start = ((bf16[16,4,1024,128]{3,2,1,0:T(8,128)(2,1)}), bf16[16,4,1024,128]{3,2,1,0:T(8,128)(2,1)}, u32[]{:S(2)}, u32[]{:S(2)}) async-start(bf16[16,4,1024,128]{3,2,1,0:T(8,128)(2,1)} %stack.2), calls=%async_computation | async-start | bytes 33554432 | tf_op jit(solution)/shard_map/all_to_all | solution.py:35
  329.1 2.7 copy-start.1
  329.1 5.0 %copy-start = (bf16[1,1024,16,128]{1,3,2,0:T(8,128)(2,1)S(1)}, bf16[1,1024,16,128]{1,3,2,0:T(8,128)(2,1)}, u32[]{:S(2)}) copy-start(bf16[1,1024,16,128]{1,3,2,0:T(8,128)(2,1)} %get-tuple-element.67) | copy-start | bytes 12582916
  331.8 6.6 %slice-start = ((s8[10485760]{0:T(1024)(128)(4,1)}), s8[4194304]{0:T(1024)(128)(4,1)S(1)}, s32[]{:S(2)}) async-start(s8[10485760]{0:T(1024)(128)(4,1)} %bitcast.63), calls=%async_computation.2 | async-start | bytes 8388608
  334.1 4.3 %slice-start.1 = ((s8[10485760]{0:T(1024)(128)(4,1)}), s8[4194304]{0:T(1024)(128)(4,1)S(1)}, s32[]{:S(2)}) async-start(s8[10485760]{0:T(1024)(128)(4,1)} %bitcast.63), calls=%async_computation.3 | async-start | bytes 8388608
  334.1 4.3 %slice-start.2 = ((s8[10485760]{0:T(1024)(128)(4,1)}), s8[2097152]{0:T(1024)(128)(4,1)S(1)}, s32[]{:S(2)}) async-start(s8[10485760]{0:T(1024)(128)(4,1)} %bitcast.63), calls=%async_computation.4 | async-start | bytes 4194304
  345.8 3.7 copy-start.2
  360.4 2.6 copy-start.3
Sparse Core Ops, SparseCore 0:
  10.3 48.6 all-gather.1
